TPU v7x, 256 devices: a whole 4x4x8 slice. The times are simulated.
256 devices in a mesh: gx: 2 (over core), gy: 4 (over x), gz: 32 (over z, y).
Axes of the slice: x: 4, y: 4, z: 8, core: 2. Of those that a mesh axis runs over, the one named last changes fastest.
Arguments:
- a_blocks: bfloat16 [4, 8, 64, 64, 2048], P('gx', 'gy', 'gz'), may hold values from -0.15625 to 0.15625
- a_cols: int32 [4, 8, 64, 32], P('gx', 'gy', 'gz'), may hold values from 0 to 26, as said below
- a_count: int32 [4, 8, 64], P('gx', 'gy', 'gz'), may hold values from 14 to 27
- p_blocks: bfloat16 [4, 8, 64, 64, 512], P('gx', 'gy', 'gz'), may hold values from -0.75 to 0.75
- p_cols: int32 [4, 8, 64, 8], P('gx', 'gy', 'gz'), may hold values from 0 to 7, as said below
- p_count: int32 [4, 8, 64], P('gx', 'gy', 'gz'), may hold values from 1 to 8
- coarse_row: int32 [2, 4, 32], P('gx', 'gy', 'gz'), may hold values from 0 to 511, as said below
Outputs:
- coarse_matrix: bfloat16 [512, 64, 8192], P(('gx', 'gy', 'gz'))
Inputs may be any that keep to these rules, and one draw needn't show every extreme that they name: `a_cols`: in each row the first a_count entries are distinct. `p_cols`: each row holds 0 to 7 once each, 0 in slot 0. `coarse_row`: values are distinct. Row r belongs to device r // 2 in mesh order; aggregate (u, v, w) goes to a row of a device with gx = u and gy = v. A device gets at most 2 aggregates, and in each group of devices with equal gx and gy one device gets exactly 2.
All inputs are finite; a program needn't handle non-finite values.
Results may differ from a plain program's by a relative error of at most 0.005.
Values may be sent and summed in bfloat16 or wider, within the bound.
No kernel may reach another device: no remote copies, remote signals or barrier semaphores. Data moves between devices by JAX's collectives and lax.ppermute only.
A program may use at most 192 MiB of HBM per device.

v0:
```python
import jax
import jax.numpy as jnp
from jax import lax
from jax.sharding import PartitionSpec as P

CLASS_PICKS = ((0,), (1, 2), (3,))


def padded(shard, sides, width):
    for axis, dim in sides:
        peers, length = (lax.axis_size(axis), shard.shape[dim])
        up = [(i, (i + 1) % peers) for i in range(peers - 1)]
        down = [(j, i) for i, j in up]
        last = lax.slice_in_dim(shard, length - width, length, axis=dim)
        initial = lax.slice_in_dim(shard, 0, width, axis=dim)
        before = lax.ppermute(last, axis, up)
        after = lax.ppermute(initial, axis, down)
        shard = jnp.concatenate([before, shard, after], axis=dim)
    return shard


def split_code(code_list):
    return (code_list // 9 - 1, code_list // 3 % 3 - 1, code_list % 3 - 1)


def axis_slot(parity, offset, code_bit):
    landing = parity + offset
    shifted = jnp.floor_divide(landing, 2)
    facing = jnp.where(jnp.remainder(landing, 2) == 0, -1, 1)
    return shifted[:, None] + code_bit[None, :] * facing[:, None]


def slot_table(parity_x, parity_y, parity_z, code_list, live_count):
    offset_x, offset_y, offset_z = split_code(code_list)
    code_range = jnp.arange(8, dtype=jnp.int32)
    slot_x = axis_slot(parity_x, offset_x, code_range % 2)
    slot_y = axis_slot(parity_y, offset_y, code_range // 2 % 2)
    slot_z = axis_slot(parity_z, offset_z, code_range // 4)
    target = (slot_x + 1) * 9 + (slot_y + 1) * 3 + (slot_z + 1)
    live = jnp.arange(code_list.shape[0], dtype=jnp.int32) < live_count
    return (target[:, :, None] == jnp.arange(28, dtype=jnp.int32)[None, None, :]) & live[
        :, None, None
    ]


def place_rows(p_blocks, p_cols, p_count):
    shape_in = p_blocks.shape
    block_size = shape_in[3]
    blocks = p_blocks.reshape(shape_in[:3] + (block_size, 8, block_size))
    code_range = jnp.arange(8, dtype=jnp.int32)
    live = code_range < p_count[..., None]
    chooser = ((p_cols[..., None] == code_range) & live[..., None]).astype(jnp.bfloat16)
    placed = jnp.einsum("xyzqc,xyzfqb->xyzfcb", chooser, blocks, preferred_element_type=jnp.float32)
    return placed.astype(jnp.bfloat16).reshape(shape_in)


def extend(field):
    return padded(field, (("gx", 0), ("gy", 1), ("gz", 2)), 1)


def coarse_sum(wide_placed, wide_product, block_size):
    extent = wide_product.shape[:3]
    groups = tuple(((size_along - 2) // 2 for size_along in extent))
    total = jnp.zeros(groups + (block_size, 5, 5, 5, block_size), jnp.float32)
    for class_x in range(3):
        for class_y in range(3):
            for class_z in range(3):
                code = (class_x != 1) * 1 + (class_y != 1) * 2 + (class_z != 1) * 4
                partial_value = jnp.zeros(groups + (block_size, 28 * block_size), jnp.float32)
                for start_x in CLASS_PICKS[class_x]:
                    for start_y in CLASS_PICKS[class_y]:
                        for start_z in CLASS_PICKS[class_z]:
                            window = (
                                slice(start_x, start_x + 2 * groups[0] - 1, 2),
                                slice(start_y, start_y + 2 * groups[1] - 1, 2),
                                slice(start_z, start_z + 2 * groups[2] - 1, 2),
                            )
                            blocks_p = wide_placed[window][
                                ..., code * block_size : (code + 1) * block_size
                            ]
                            blocks_ap = wide_product[window]
                            partial_value = partial_value + jnp.einsum(
                                "uvwfa,uvwfe->uvwae",
                                blocks_p,
                                blocks_ap,
                                preferred_element_type=jnp.float32,
                            )
                partial_value = partial_value.reshape(groups + (block_size, 28, block_size))[
                    ..., :27, :
                ]
                partial_value = partial_value.reshape(groups + (block_size, 3, 3, 3, block_size))
                total = total.at[
                    :,
                    :,
                    :,
                    :,
                    class_x : class_x + 3,
                    class_y : class_y + 3,
                    class_z : class_z + 3,
                    :,
                ].add(partial_value)
    return total


def local(a_blocks, a_cols, a_count, p_blocks, p_cols, p_count, coarse_row):
    box_x, box_y, box_z, block_size = a_blocks.shape[:4]
    slot_count = a_cols.shape[3]
    row_count = box_x * box_y * box_z
    placed = place_rows(p_blocks, p_cols, p_count)
    wide_placed = extend(placed)
    flat_placed = wide_placed.reshape(-1, block_size, 8 * block_size)
    row_ids = jnp.arange(row_count, dtype=jnp.int32)
    local_x = row_ids // (box_y * box_z)
    local_y = row_ids // box_z % box_y
    local_z = row_ids % box_z

    def one_row(row_item):
        row_blocks, code_list, live_count, at_x, at_y, at_z = row_item
        offset_x, offset_y, offset_z = split_code(code_list)
        flat_index = ((at_x + offset_x + 1) * (box_y + 2) + (at_y + offset_y + 1)) * (box_z + 2) + (
            at_z + offset_z + 1
        )
        pieces = jnp.take(flat_placed, flat_index, axis=0).reshape(
            slot_count, block_size, 8, block_size
        )
        chooser = slot_table(at_x % 2, at_y % 2, at_z % 2, code_list, live_count)
        row_split = row_blocks.reshape(block_size, slot_count, block_size)
        partial_value = jnp.einsum(
            "akc,kcqb->kaqb", row_split, pieces, preferred_element_type=jnp.float32
        )
        summed = jnp.einsum(
            "kqe,kaqb->aeb",
            chooser.astype(jnp.float32),
            partial_value,
            precision=lax.Precision.HIGHEST,
        )
        return summed.reshape(block_size, 28 * block_size).astype(jnp.bfloat16)

    product = lax.map(
        one_row,
        (
            a_blocks.reshape(row_count, block_size, slot_count * block_size),
            a_cols.reshape(row_count, slot_count),
            a_count.reshape(row_count),
            local_x,
            local_y,
            local_z,
        ),
    )
    product = product.reshape(box_x, box_y, box_z, block_size, 28 * block_size)
    wide_product = extend(product)
    total = coarse_sum(wide_placed, wide_product, block_size)
    coarse_rows = total.reshape(-1, block_size, 125 * block_size)
    coarse_rows = jnp.pad(coarse_rows, ((0, 0), (0, 0), (0, 3 * block_size))).astype(jnp.bfloat16)
    aggregate_count = coarse_rows.shape[0]
    row_targets = coarse_row.reshape(aggregate_count)
    capacity = 2 * aggregate_count
    group_size = lax.axis_size("gz")
    group_base = (lax.axis_index("gx") * lax.axis_size("gy") + lax.axis_index("gy")) * group_size
    slot_base = (group_base + lax.axis_index("gz")) * capacity
    owner_local = row_targets // capacity - group_base
    owner_hits = owner_local[None, :] == jnp.arange(group_size, dtype=jnp.int32)[:, None]
    outgoing = jnp.where(
        owner_hits[:, :, None, None], coarse_rows[None], jnp.zeros((), jnp.bfloat16)
    )
    outgoing = outgoing.reshape(group_size * aggregate_count, block_size, 128 * block_size)
    outgoing_targets = jnp.where(owner_hits, row_targets[None, :], -1).reshape(
        group_size * aggregate_count
    )
    arrived_rows, arrived_targets = (
        lax.all_to_all(outgoing, "gz", split_axis=0, concat_axis=0, tiled=True),
        lax.all_to_all(outgoing_targets, "gz", split_axis=0, concat_axis=0, tiled=True),
    )
    matches = arrived_targets[:, None] == slot_base + jnp.arange(capacity, dtype=jnp.int32)[None, :]
    chosen = jnp.einsum(
        "nt,nab->tab",
        matches.astype(jnp.bfloat16),
        arrived_rows,
        preferred_element_type=jnp.float32,
    )
    return chosen.astype(jnp.bfloat16)


def solution(mesh):
    in_specs = (
        P("gx", "gy", "gz", None, None),
        P("gx", "gy", "gz", None),
        P("gx", "gy", "gz"),
        P("gx", "gy", "gz", None, None),
        P("gx", "gy", "gz", None),
        P("gx", "gy", "gz"),
        P("gx", "gy", "gz"),
    )
    out_specs = P(("gx", "gy", "gz"), None, None)
    return jax.shard_map(local, mesh=mesh, in_specs=in_specs, out_specs=out_specs, check_vma=False)
```

profile of v0, /device:TPU:2, one launch (start us, length us, event | category | flops | bytes accessed | tf_op | source)
XLA Modules:
  0.0 1476.3 jit_solution(13244560726575752994)
XLA Ops:
  9.6 3.4 collective-permute-start.2
  13.0 2.5 collective-permute-start.3
  15.5 9.9 collective-permute-done.2
  25.4 3.1 collective-permute-done.3
  30.3 4.5 collective-permute-start.4
  37.3 12.5 all-to-all-start
  51.2 4.6 collective-permute-done.4
  55.8 5.1 collective-permute-done.5
  60.9 3.5 pad_maximum_fusion.1
  64.4 272.3 %while.40 = (s32[]{:T(128)}, bf16[8,64,1792]{2,1,0:T(8,128)(2,1)}, bf16[8,64,2048]{2,1,0:T(8,128)(2,1)}, s32[8]{0:T(128)S(1)}, s32[8,32]{1,0:T(8,128)}, /*index=...) while((s32[]{:T(128)}, bf16[8,64,1792]{2,1,0:T(8,128)(2,1)}, ...), condition=%wide.region_1.2_spmd, body=%wide.region_0.1_spmd.sunk | while | flops 487726656 | bytes 21342824 | solution.py:139
  79.2 2.9 gather_fusion
  82.1 3.7 gather.15
  85.8 3.5 fusion.151
  89.3 7.9 fusion.152
  113.2 2.9 gather_fusion
  116.1 3.7 gather.15
  119.8 3.5 fusion.151
  123.3 7.9 fusion.152
  147.2 2.9 gather_fusion
  150.1 3.7 gather.15
  153.8 3.5 fusion.151
  157.2 7.9 fusion.152
  181.2 2.9 gather_fusion
  184.0 3.7 gather.15
  187.7 3.5 fusion.151
  191.2 7.9 fusion.152
  215.2 2.9 gather_fusion
  218.0 3.7 gather.15
  221.7 3.5 fusion.151
  225.2 7.9 fusion.152
  249.1 2.9 gather_fusion
  252.0 3.7 gather.15
  255.7 3.5 fusion.151
  259.2 7.9 fusion.152
  283.1 2.9 gather_fusion
  286.0 3.7 gather.15
  289.7 3.5 fusion.151
  293.2 7.9 fusion.152
  317.1 2.9 gather_fusion
  320.0 3.7 gather.15
  323.7 3.5 fusion.151
  327.2 7.9 fusion.152
  336.7 3.0 fusion.128
  342.0 4.1 collective-permute-start.6
  347.8 2.4 reshape.3050
  350.2 2.7 copy.196
  354.4 2.2 fusion.126
  356.6 3.1 collective-permute-start.8
  359.8 3.9 collective-permute-start.9
  369.3 2.7 copy.207
  378.5 2.7 copy.185
  381.2 18.0 %collective-permute-done.8 = bf16[4,1,2,64,1792]{4,3,2,1,0:T(8,128)(2,1)} collective-permute-done((bf16[4,1,2,64,1792]{4,3,2,1,0:T(8,128)(2,1)}, bf16[4,1,2,64,1792]{4,3,2,1,0:T(8,128)(2,1)}, u32[]{:S(2)}, u32[]{:S(2)}) %collective-permute-start.8) | collective-permute-done | bytes 1835040 | tf_op jit(solution)/shard_map/ppermute | solution.py:16
  399.2 2.8 collective-permute-done.9
  402.0 3.5 pad_maximum_fusion
  405.5 3.4 fusion.125
  441.4 6.5 collective-permute-start.10
  447.9 41.7 %collective-permute-done.11 = bf16[4,4,1,64,1792]{4,3,2,1,0:T(8,128)(2,1)} collective-permute-done((bf16[4,4,1,64,1792]{4,3,2,1,0:T(8,128)(2,1)}, bf16[4,4,1,64,1792]{4,3,2,1,0:T(8,128)(2,1)}, u32[]{:S(2)}, u32[]{:S(2)}) %collective-permute-start.11) | collective-permute-done | bytes 3670048 | tf_op jit(solution)/shard_map/ppermute | solution.py:17
  559.2 2.1 add_dynamic-update-slice_fusion
  570.2 4.7 copy.214
  577.7 11.1 broadcast_select_fusion
  588.8 17.0 %all-to-all-start.1 = ((bf16[32,64,8192]{2,1,0:T(8,128)(2,1)}), bf16[32,64,8192]{2,1,0:T(8,128)(2,1)}, u32[]{:S(2)}, u32[]{:S(2)}) async-start(bf16[32,64,8192]{2,1,0:T(8,128)(2,1)} %broadcast_select_fusion), calls=%async_computation.1 | async-start | bytes 67108864 | tf_op jit(solution)/shard_map/all_to_all | solution.py:171
  606.5 792.0 %all-to-all-done.1 = bf16[32,64,8192]{2,1,0:T(8,128)(2,1)} async-done(((bf16[32,64,8192]{2,1,0:T(8,128)(2,1)}), bf16[32,64,8192]{2,1,0:T(8,128)(2,1)}, u32[]{:S(2)}, u32[]{:S(2)}) %all-to-all-start.1) | async-done | bytes 33554464 | tf_op jit(solution)/shard_map/all_to_all | solution.py:171
  1398.5 75.1 %fusion.40 = bf16[2,64,8192]{2,0,1:T(2,128)(2,1)S(1)} fusion(bf16[32,64,8192]{2,1,0:T(8,128)(2,1)} %all-to-all-done.1, s32[32]{0:T(128)S(1)} %reduce.54, s32[2]{0:T(128)S(1)} %iota_add_fusion), kind=kOutput, calls=%fused_computation.90 | convolution fusion | flops 68157504 | bytes 35651720 | tf_op jit(solution)/shard_map/nt,nab->tab/dot_general | solution.py:175
  1473.6 2.5 copy.217
  (397 shorter events, 227.6 us)
Async XLA Ops:
  3.9 4.0 collective-permute-start
  6.0 3.4 collective-permute-start.1
  9.4 3.5 copy-start.27
  9.6 15.9 %collective-permute-start.2 = (bf16[4,1,2,64,512]{4,3,2,1,0:T(8,128)(2,1)S(1)}, bf16[4,1,2,64,512]{4,3,2,1,0:T(8,128)(2,1)S(1)}, u32[]{:S(2)}, u32[]{:S(2)}) collective-permute-start(bf16[4,1,2,64,512]{4,3,2,1,0:T(8,128)(2,1)S(1)} %get-tuple-element.581), channel_id=1, source_target_pairs={{0,32},{32,64},{64,96},{1,33},{33,65},{65,97},{2,34},{34,66},{66,9... | collective-permute-start | bytes 1572872 | tf_op jit(solution)/shard_map/ppermute | solution.py:16
  13.0 36.8 %copy-start.28 = (s32[2,2,2]{2,1,0:T(2,128)S(1)}, s32[2,2,2]{2,1,0:T(2,128)}, u32[]{:S(2)}) copy-start(s32[2,2,2]{2,1,0:T(2,128)} %param.65) | copy-start | bytes 100
  13.0 15.6 %collective-permute-start.3 = (bf16[4,1,2,64,512]{4,3,2,1,0:T(8,128)(2,1)S(1)}, bf16[4,1,2,64,512]{4,3,2,1,0:T(8,128)(2,1)S(1)}, u32[]{:S(2)}, u32[]{:S(2)}) collective-permute-start(bf16[4,1,2,64,512]{4,3,2,1,0:T(8,128)(2,1)S(1)} %get-tuple-element.582), channel_id=1, source_target_pairs={{32,0},{64,32},{96,64},{33,1},{65,33},{97,65},{34,2},{66,34},{98,6... | collective-permute-start | bytes 1572872 | tf_op jit(solution)/shard_map/ppermute | solution.py:17
  25.4 35.5 %copy-start.26 = (bf16[4,1,2,64,512]{4,3,2,1,0:T(8,128)(2,1)}, bf16[4,1,2,64,512]{4,3,2,1,0:T(8,128)(2,1)S(1)}, u32[]{:S(2)}) copy-start(bf16[4,1,2,64,512]{4,3,2,1,0:T(8,128)(2,1)S(1)} %collective-permute-done.2) | copy-start | bytes 1572868
  28.6 32.3 %copy-start.25 = (bf16[4,1,2,64,512]{4,3,2,1,0:T(8,128)(2,1)}, bf16[4,1,2,64,512]{4,3,2,1,0:T(8,128)(2,1)S(1)}, u32[]{:S(2)}) copy-start(bf16[4,1,2,64,512]{4,3,2,1,0:T(8,128)(2,1)S(1)} %collective-permute-done.3) | copy-start | bytes 1572868
  30.3 25.5 %collective-permute-start.4 = (bf16[4,4,1,64,512]{4,3,2,1,0:T(8,128)(2,1)}, bf16[4,4,1,64,512]{4,3,2,1,0:T(8,128)(2,1)}, u32[]{:S(2)}, u32[]{:S(2)}) collective-permute-start(bf16[4,4,1,64,512]{4,3,2,1,0:T(8,128)(2,1)} %get-tuple-element.577), channel_id=1, source_target_pairs={{0,1},{1,2},{2,3},{3,4},{4,5},{5,6},{6,7},{7,8},{8,9},{9,10},{10,1... | collective-permute-start | bytes 3145736 | tf_op jit(solution)/shard_map/ppermute | solution.py:16
  34.7 26.1 %collective-permute-start.5 = (bf16[4,4,1,64,512]{4,3,2,1,0:T(8,128)(2,1)}, bf16[4,4,1,64,512]{4,3,2,1,0:T(8,128)(2,1)}, u32[]{:S(2)}, u32[]{:S(2)}) collective-permute-start(bf16[4,4,1,64,512]{4,3,2,1,0:T(8,128)(2,1)} %get-tuple-element.578), channel_id=1, source_target_pairs={{1,0},{2,1},{3,2},{4,3},{5,4},{6,5},{7,6},{8,7},{9,8},{10,9},{11,1... | collective-permute-start | bytes 3145736 | tf_op jit(solution)/shard_map/ppermute | solution.py:17
  37.3 551.5 %all-to-all-start = ((s32[32,1,1]{2,1,0:T(1,128)}), s32[32,1,1]{2,1,0:T(1,128)S(1)}, u32[]{:S(2)}, u32[]{:S(2)}) async-start(s32[32,1,1]{2,1,0:T(1,128)} %compare_select_fusion.16), calls=%async_computation | async-start | bytes 32768 | tf_op jit(solution)/shard_map/all_to_all | solution.py:172
  336.7 3.0 copy-start
  340.7 12.3 collective-permute-start.7
  342.0 11.0 collective-permute-start.6
  356.6 42.5 %collective-permute-start.8 = (bf16[4,1,2,64,1792]{4,3,2,1,0:T(8,128)(2,1)}, bf16[4,1,2,64,1792]{4,3,2,1,0:T(8,128)(2,1)}, u32[]{:S(2)}, u32[]{:S(2)}) collective-permute-start(bf16[4,1,2,64,1792]{4,3,2,1,0:T(8,128)(2,1)} %get-tuple-element.575), channel_id=1, source_target_pairs={{0,32},{32,64},{64,96},{1,33},{33,65},{65,97},{2,34},{34,66},{66,9... | collective-permute-start | bytes 5505032 | tf_op jit(solution)/shard_map/ppermute | solution.py:16
  359.8 42.3 %collective-permute-start.9 = (bf16[4,1,2,64,1792]{4,3,2,1,0:T(8,128)(2,1)}, bf16[4,1,2,64,1792]{4,3,2,1,0:T(8,128)(2,1)}, u32[]{:S(2)}, u32[]{:S(2)}) collective-permute-start(bf16[4,1,2,64,1792]{4,3,2,1,0:T(8,128)(2,1)} %get-tuple-element.576), channel_id=1, source_target_pairs={{32,0},{64,32},{96,64},{33,1},{65,33},{97,65},{34,2},{66,34},{98,6... | collective-permute-start | bytes 5505032 | tf_op jit(solution)/shard_map/ppermute | solution.py:17
  408.9 80.7 %collective-permute-start.11 = (bf16[4,4,1,64,1792]{4,3,2,1,0:T(8,128)(2,1)}, bf16[4,4,1,64,1792]{4,3,2,1,0:T(8,128)(2,1)}, u32[]{:S(2)}, u32[]{:S(2)}) collective-permute-start(bf16[4,4,1,64,1792]{4,3,2,1,0:T(8,128)(2,1)} %get-tuple-element.565), channel_id=1, source_target_pairs={{1,0},{2,1},{3,2},{4,3},{5,4},{6,5},{7,6},{8,7},{9,8},{10,9},{11,1... | collective-permute-start | bytes 11010056 | tf_op jit(solution)/shard_map/ppermute | solution.py:17
  441.4 82.7 %collective-permute-start.10 = (bf16[4,4,1,64,1792]{4,3,2,1,0:T(8,128)(2,1)}, bf16[4,4,1,64,1792]{4,3,2,1,0:T(8,128)(2,1)}, u32[]{:S(2)}, u32[]{:S(2)}) collective-permute-start(bf16[4,4,1,64,1792]{4,3,2,1,0:T(8,128)(2,1)} %get-tuple-element.566), channel_id=1, source_target_pairs={{0,1},{1,2},{2,3},{3,4},{4,5},{5,6},{6,7},{7,8},{8,9},{9,10},{10,1... | collective-permute-start | bytes 11010056 | tf_op jit(solution)/shard_map/ppermute | solution.py:16
  492.6 4.3 copy-start.1
  496.9 0.9 copy-start.2
  499.5 6.1 copy-start.3
  527.0 4.4 copy-start.4
  531.4 1.0 copy-start.5
  556.2 1.2 copy-start.15
  556.7 1.2 slice-start.2
  557.2 1.3 copy-start.24
  557.3 1.4 copy-start.11
  557.9 1.3 copy-start.21
  558.5 2.9 slice-start.4
  558.7 2.9 copy-start.16
  559.2 2.6 slice-start.1
  561.3 1.2 copy-start.22
  561.6 1.2 copy-start.13
  561.9 1.3 copy-start.18
  562.5 1.3 copy-start.23
  562.8 1.3 copy-start.8
  563.2 1.3 copy-start.19
  564.1 1.2 copy-start.14
  564.4 1.2 copy-start.20
  564.7 1.3 copy-start.7
  565.4 1.3 copy-start.10
  565.7 1.3 copy-start.6
  566.7 1.2 copy-start.9
  566.9 1.2 copy-start.17
  567.2 1.3 slice-start.3
  567.9 1.3 copy-start.12
  568.2 1.3 slice-start
  574.9 2.8 copy-start.29
  588.8 809.7 %all-to-all-start.1 = ((bf16[32,64,8192]{2,1,0:T(8,128)(2,1)}), bf16[32,64,8192]{2,1,0:T(8,128)(2,1)}, u32[]{:S(2)}, u32[]{:S(2)}) async-start(bf16[32,64,8192]{2,1,0:T(8,128)(2,1)} %broadcast_select_fusion), calls=%async_computation.1 | async-start | bytes 67108864 | tf_op jit(solution)/shard_map/all_to_all | solution.py:171
where the time goes:
time: 1500 us; the launch traced here: 1480 us
  waiting for transfers between devices  879 us (59%)
  matrix products  240 us (16%)
  local copies, waits for them, and re-layouts  173 us (12%)
  other arithmetic  72.3 us (5%)
  starting transfers between devices  64.3 us (4%)
  loops' own time  46.3 us (3%)
    all_to_all x1, waiting for transfers between devices, local(): lax.all_to_all(outgoing, 'gz', split_axis=0, concat_axis=0, tiled=True)  792 us
    dot_general x1, matrix products, local(): jnp.einsum('nt,nab->tab', matches.astype(jnp.bfloat16), arrived_rows, pre...  75.1 us
    dot_general x64, matrix products, coarse_sum(): jnp.einsum('uvwfa,uvwfe->uvwae', blocks_p, blocks_ap, preferred_element_t...  72.2 us
    dot_general x8, matrix products, one_row(): jnp.einsum('kqe,kaqb->aeb', chooser.astype(jnp.float32), partial_value, p...  63.5 us
    ppermute x6, waiting for transfers between devices, padded(): after = lax.ppermute(initial, axis, down)  54.3 us
    gather x16, local copies, waits for them, and re-layouts, one_row(): jnp.take(flat_placed, flat_index, axis=0)  52.5 us
    another operation x1, loops' own time, local(): lax.map(one_row, (a_blocks.reshape(row_count, block_size, slot_count * bl...  46.3 us
    slice x32, local copies, waits for them, and re-layouts, coarse_sum(): partial_value.reshape(groups + (block_size, 28, block_size))[..., :27, :]  32.6 us
  transfers between devices with their start and end apart: 14, of which 9 were waited for; matrix products, arithmetic and copies ran while one was open for 27% of the time, Pallas kernels for 0%

commit v1 on v0

v1 whole, which is shorter than its diff:
```python
import jax
import jax.numpy as jnp
from jax import lax
from jax.experimental import pallas as pl
from jax.experimental.pallas import tpu as pltpu
from jax.sharding import PartitionSpec as P

F32 = jnp.float32
BF16 = jnp.bfloat16
INTERPRET = False
VMEM = pl.BlockSpec(memory_space=pltpu.VMEM)
SMEM = pl.BlockSpec(memory_space=pltpu.SMEM)


def lanes_of(shape):
    return lax.broadcasted_iota(jnp.int32, shape, 1)


def half_turn(tile):
    return pltpu.roll(tile, 64, 1)


def doubled(pair, low):
    turned = half_turn(pair)
    return jnp.where(low, pair, turned), jnp.where(low, turned, pair)


def sort_kernel(spot_ref, p_ref, out_ref, sorted_ref):
    low = lanes_of((64, 128)) < 64
    half_of = lanes_of((64, 128)) // 64
    sorted_ref[...] = jnp.zeros(sorted_ref.shape, F32)
    for row in range(8):
        for slot_pair in range(4):
            pair = p_ref[row, :, 128 * slot_pair : 128 * slot_pair + 128].astype(F32)
            for side, block in enumerate(doubled(pair, low)):
                spot = spot_ref[row * 8 + slot_pair * 2 + side]
                at = row * 5 + spot // 2
                sorted_ref[at] = sorted_ref[at] + jnp.where(half_of == spot % 2, block, 0.0)
        for place in range(4):
            out_ref[row, :, 128 * place : 128 * place + 128] = sorted_ref[row * 5 + place].astype(
                BF16
            )


def product_kernel(spot_ref, a_ref, w_ref, own_ref, out_ref, left_ref, acc_ref, plain_ref, turn_ref, outer_ref, inner_ref):
    low = lanes_of((64, 128)) < 64
    half_of = lanes_of((64, 128)) // 64
    left_ref[...] = jnp.zeros(left_ref.shape, BF16)
    acc_ref[...] = jnp.zeros(acc_ref.shape, F32)
    outer_ref[...] = jnp.zeros(outer_ref.shape, BF16)
    inner_ref[...] = jnp.zeros(inner_ref.shape, BF16)

    def fill(row, carry):
        start = pl.multiple_of(row * 64, 64)
        for slot_pair in range(16):
            pair = a_ref[row, :, 128 * slot_pair : 128 * slot_pair + 128].astype(F32)
            for side, block in enumerate(doubled(pair, low)):
                spot = spot_ref[row * 32 + slot_pair * 2 + side]
                at = spot // 2
                piece = jnp.where(half_of == spot % 2, block, 0.0)
                old = left_ref[at, pl.ds(start, 64), :].astype(F32)
                left_ref[at, pl.ds(start, 64), :] = (old + piece).astype(BF16)
        return carry

    lax.fori_loop(0, 8, fill, 0)

    low_tall = lanes_of((512, 128)) < 64
    for hx in range(2):
        for hy in range(2):
            for hz in range(2):
                left = jnp.concatenate(
                    [
                        left_ref[((2 * hx + jx) * 4 + 2 * hy + jy) * 2 + hz]
                        for jx in range(2)
                        for jy in range(2)
                    ],
                    axis=1,
                )
                right = jnp.concatenate(
                    [
                        w_ref[((2 * hx + jx) * 4 + 2 * hy + jy) * 4 + 2 * hz + jz]
                        for jx in range(2)
                        for jy in range(2)
                        for jz in range(2)
                    ],
                    axis=0,
                )
                result = jnp.dot(left, right, preferred_element_type=F32)
                for bx in range(2):
                    for by in range(2):
                        at = (hx + bx) * 3 + hy + by
                        lane = (bx * 2 + by) * 128
                        piece = result[:, lane : lane + 128]
                        if hz == 0:
                            acc_ref[at, :, 0:128] += piece
                        else:
                            turned = half_turn(piece)
                            acc_ref[at, :, 0:128] += jnp.where(low_tall, 0.0, turned)
                            acc_ref[at, :, 128:256] += jnp.where(low_tall, turned, 0.0)
    for at in range(9):
        near = acc_ref[at, :, 0:128]
        far = acc_ref[at, :, 128:256]
        plain_ref[at, :, 0:128] = near.astype(BF16)
        plain_ref[at, :, 128:256] = far.astype(BF16)
        near_turned = half_turn(near)
        far_turned = half_turn(far)
        turn_ref[at, :, 0:128] = jnp.where(low_tall, 0.0, near_turned).astype(BF16)
        turn_ref[at, :, 128:256] = jnp.where(low_tall, near_turned, far_turned).astype(BF16)

    for vx in range(2):
        for vy in range(2):
            lane = (vx * 2 + vy) * 128
            for bx in range(2):
                for by in range(2):
                    group = (vx + bx) * 3 + vy + by
                    place = (bx * 2 + by) * 128
                    block = jnp.concatenate(
                        [
                            own_ref[(vx * 2 + vy) * 2 + vz, :, place : place + 128]
                            for vz in range(2)
                        ],
                        axis=0,
                    )
                    flipped = block.astype(F32).T
                    first, second = flipped[0:64], flipped[64:128]
                    outer_ref[group * 128 : group * 128 + 64, lane : lane + 128] = jnp.where(
                        low, first, 0.0
                    ).astype(BF16)
                    outer_ref[group * 128 + 64 : group * 128 + 128, lane : lane + 128] = jnp.where(
                        low, 0.0, second
                    ).astype(BF16)
                    inner_ref[group * 64 : group * 64 + 64, lane : lane + 128] = jnp.where(
                        low, second, first
                    ).astype(BF16)

    for at in range(9):
        lane = at * 256
        outer = jnp.dot(outer_ref[...], plain_ref[at], preferred_element_type=F32).astype(BF16)
        inner = jnp.dot(inner_ref[...], turn_ref[at], preferred_element_type=F32).astype(BF16)
        for group in range(9):
            out_ref[group, 0:128, lane : lane + 256] = outer[group * 128 : group * 128 + 128]
            out_ref[group, 128:192, lane : lane + 256] = inner[group * 64 : group * 64 + 64]


def finish_kernel(side_ref, own_ref, before_ref, after_ref, out_ref):
    low = lanes_of((64, 128)) < 64
    per_chunk = out_ref.shape[2] // 128

    def store(tile, value):
        lane = tile % per_chunk * 128
        out_ref[tile // per_chunk, :, lane : lane + 128] = value.astype(BF16)

    def column(ref, at, part):
        return ref[:, at * 256 + part * 128 : at * 256 + part * 128 + 128].astype(F32)

    tiles = []
    for pair in range(10):
        parts = []
        for at in (2 * pair, 2 * pair + 1):
            parts.append(
                (
                    column(own_ref, at, 0) + column(before_ref, at, 0),
                    column(own_ref, at, 1) + column(before_ref, at, 1) + column(after_ref, at, 0),
                    column(after_ref, at, 1),
                )
            )
        turned = [half_turn(tile) for tile in parts[1]]
        tiles += [
            parts[0][0],
            parts[0][1],
            jnp.where(low, parts[0][2], turned[0]),
            jnp.where(low, turned[0], turned[1]),
            jnp.where(low, turned[1], turned[2]),
        ]
    out_ref[...] = jnp.zeros(out_ref.shape, BF16)

    @pl.when(side_ref[0] == 1)
    def _():
        for at in range(50):
            store(at, tiles[at])

    @pl.when(side_ref[0] == 0)
    def _():
        last = jnp.zeros((64, 128), F32)
        for at in range(50):
            turned = half_turn(tiles[at])
            store(12 + at, jnp.where(low, last, turned))
            last = turned
        store(62, jnp.where(low, last, 0.0))


def pick_kernel(from_ref, live_ref, rows_ref, out_ref):
    def step(at, carry):
        @pl.when(live_ref[at] == 1)
        def _():
            out_ref[at] = rows_ref[from_ref[at]]

        @pl.when(live_ref[at] == 0)
        def _():
            out_ref[at] = jnp.zeros(out_ref.shape[1:], BF16)

        return carry

    lax.fori_loop(0, out_ref.shape[0], step, 0)


def call(kernel, out_shape, in_specs, scratch=()):
    return pl.pallas_call(
        kernel,
        out_shape=jax.ShapeDtypeStruct(out_shape, BF16),
        in_specs=in_specs,
        out_specs=VMEM,
        scratch_shapes=list(scratch),
        compiler_params=pltpu.CompilerParams(vmem_limit_bytes=58 * 1024 * 1024),
        interpret=INTERPRET,
    )


def chain(axis):
    size = lax.axis_size(axis)
    return [(i, i + 1) for i in range(size - 1)], [(i + 1, i) for i in range(size - 1)]


def local(a_blocks, a_cols, a_count, p_blocks, p_cols, p_count, coarse_row):
    side = lax.axis_index("gx")
    lower = side == 0
    group_size = lax.axis_size("gz")
    swap = [(0, 1), (1, 0)]
    up_y, down_y = chain("gy")
    up_z, down_z = chain("gz")

    group_base = (side * lax.axis_size("gy") + lax.axis_index("gy")) * group_size * 2
    targets = lax.all_gather(coarse_row.reshape(1), "gz", tiled=True) - group_base
    hits = jnp.arange(2 * group_size, dtype=jnp.int32)[:, None] == targets[None, :]
    source = jnp.sum(
        jnp.where(hits, jnp.arange(group_size, dtype=jnp.int32)[None, :], 0), axis=1
    ).astype(jnp.int32)
    live = jnp.any(hits, axis=1).astype(jnp.int32)

    row_ids = jnp.arange(8, dtype=jnp.int32)[:, None]
    row_x, row_y, row_z = row_ids // 4, row_ids // 2 % 2, row_ids % 2

    codes = p_cols.reshape(8, 8)
    place_x = codes % 2 ^ (1 - row_x)
    place_y = codes // 2 % 2 ^ (1 - row_y)
    place_z = codes // 4 ^ (1 - row_z)
    p_spot = jnp.where(
        jnp.arange(8, dtype=jnp.int32)[None, :] < p_count.reshape(8, 1),
        place_x * 4 + place_y * 2 + place_z,
        8,
    )
    placed = call(sort_kernel, (8, 64, 512), [SMEM, VMEM], [pltpu.VMEM((40, 64, 128), F32)])(
        p_spot.reshape(-1), p_blocks.reshape(8, 64, 512)
    )

    wide = placed.reshape(2, 2, 2, 64, 512)
    wide = jnp.concatenate(
        [
            lax.ppermute(wide[:, :, 1:2], "gz", up_z),
            wide,
            lax.ppermute(wide[:, :, 0:1], "gz", down_z),
        ],
        axis=2,
    )
    wide = jnp.concatenate(
        [
            lax.ppermute(wide[:, 1:2], "gy", up_y),
            wide,
            lax.ppermute(wide[:, 0:1], "gy", down_y),
        ],
        axis=1,
    )
    facing = lax.ppermute(jnp.where(lower, wide[1:2], wide[0:1]), "gx", swap)
    nothing = jnp.zeros((), BF16)
    wide = jnp.concatenate(
        [jnp.where(lower, nothing, facing), wide, jnp.where(lower, facing, nothing)], axis=0
    )

    neighbours = a_cols.reshape(8, 32)
    at_x = row_x + neighbours // 9
    at_y = row_y + neighbours // 3 % 3
    at_z = row_z + neighbours % 3
    a_spot = jnp.where(
        jnp.arange(32, dtype=jnp.int32)[None, :] < a_count.reshape(8, 1),
        (at_x * 4 + at_y) * 4 + at_z,
        64,
    )
    parts = call(
        product_kernel,
        (9, 192, 2304),
        [SMEM, VMEM, VMEM, VMEM],
        [
            pltpu.VMEM((33, 512, 128), BF16),
            pltpu.VMEM((9, 512, 256), F32),
            pltpu.VMEM((9, 512, 256), BF16),
            pltpu.VMEM((9, 512, 256), BF16),
            pltpu.VMEM((1152, 512), BF16),
            pltpu.VMEM((576, 512), BF16),
        ],
    )(
        a_spot.reshape(-1),
        a_blocks.reshape(8, 64, 2048),
        wide.reshape(64, 64, 512),
        placed,
    )
    parts = parts.reshape(3, 3, 192, 2304)

    own = parts[1]
    came = lax.ppermute(jnp.where(lower, parts[2], parts[0]), "gx", swap)
    first = jnp.where(lower, own, came).astype(F32)
    second = jnp.where(lower, came, own).astype(F32)
    summed = jnp.pad(first, ((0, 0), (0, 0), (0, 768))) + jnp.pad(
        second, ((0, 0), (0, 0), (768, 0))
    )
    summed = summed.astype(BF16)

    before = lax.ppermute(summed[2], "gy", up_y)
    after = lax.ppermute(summed[0], "gy", down_y)

    def widened(field, shift):
        field = field.reshape(192, 4, 768).astype(F32)
        return jnp.pad(field, ((0, 0), (0, 0), (256 * shift, 512 - 256 * shift)))

    summed = widened(before, 0) + widened(summed[1], 1) + widened(after, 2)
    summed = summed.astype(BF16).reshape(192, 5120)

    before = lax.ppermute(summed[64:128], "gz", up_z)
    after = lax.ppermute(summed[0:64], "gz", down_z)
    width = 8192 // group_size
    chunks = call(finish_kernel, (group_size, 64, width), [SMEM, VMEM, VMEM, VMEM])(
        side.astype(jnp.int32).reshape(1), summed[128:192], before, after
    )

    rows = lax.all_to_all(chunks, "gz", split_axis=0, concat_axis=0, tiled=True)
    picked = call(pick_kernel, (2 * group_size, 64, width), [SMEM, SMEM, VMEM])(source, live, rows)
    landed = lax.all_to_all(picked, "gz", split_axis=0, concat_axis=0, tiled=True)
    landed = landed.reshape(group_size, 2, 64, width)
    return jnp.transpose(landed, (1, 2, 0, 3)).reshape(2, 64, 8192)


def solution(mesh):
    in_specs = (
        P("gx", "gy", "gz", None, None),
        P("gx", "gy", "gz", None),
        P("gx", "gy", "gz"),
        P("gx", "gy", "gz", None, None),
        P("gx", "gy", "gz", None),
        P("gx", "gy", "gz"),
        P("gx", "gy", "gz"),
    )
    out_specs = P(("gx", "gy", "gz"), None, None)
    return jax.shard_map(local, mesh=mesh, in_specs=in_specs, out_specs=out_specs, check_vma=False)
```

time: 1500 us -> 247 us (0.16); the launches traced: 1480 us -> 246 us
  waiting for transfers between devices: 879 us -> 63.6 us
  matrix products: 240 us -> 0 us
  local copies, waits for them, and re-layouts: 173 us -> 18.4 us
  blocking collectives: 0 us -> 84.5 us
  other arithmetic: 72.3 us -> 15 us
  loops' own time: 46.3 us -> 0 us
  starting transfers between devices: 64.3 us -> 38 us
  Pallas kernels: 0 us -> 26 us
    all_to_all x2 -> x1, waiting for transfers between devices: 792 us -> 0.01 us  [local(): rows = lax.all_to_all(chunks, 'gz', split_axis=0, concat_axis=0, tiled=True)]
    dot_general x82 -> x0, matrix products: 240 us -> none  [the longest x1 75.1 us: local(): jnp.einsum('nt,nab->tab', matches.astype(jnp.bfloat16), arrived_rows, pre...]
    all_to_all x0 -> x1, blocking collectives: none -> 56 us  [local(): lax.all_to_all(picked, 'gz', split_axis=0, concat_axis=0, tiled=True)]
    gather x16 -> x0, local copies, waits for them, and re-layouts: 52.5 us -> none  [one_row(): jnp.take(flat_placed, flat_index, axis=0)]
    another operation x1 -> x0, loops' own time: 46.3 us -> none  [local(): lax.map(one_row, (a_blocks.reshape(row_count, block_size, slot_count * bl...]
    slice x40 -> x3, local copies, waits for them, and re-layouts: 43.5 us -> 1.87 us  [the longest x1 1.12 us: local(): wide[:, :, 1:2]]
    unnamed x0 -> x1, blocking collectives: none -> 28.6 us
    dynamic_slice x40 -> x0, local copies, waits for them, and re-layouts: 27.1 us -> none  [local(): lax.map(one_row, (a_blocks.reshape(row_count, block_size, slot_count * bl...]
  transfers between devices with their start and end apart: 14 -> 11, of which waited for: 9 -> 9; matrix products, arithmetic and copies ran while one was open for 27% -> 4% of each run, Pallas kernels for 0% -> 0%
where the time goes in v1:
time: 247 us; the launch traced here: 246 us
  blocking collectives  84.5 us (34%)
  waiting for transfers between devices  63.6 us (26%)
  starting transfers between devices  38 us (15%)
  Pallas kernels  26 us (11%)
  local copies, waits for them, and re-layouts  18.4 us (7%)
  other arithmetic  15 us (6%)
    all_to_all x1, blocking collectives, local(): lax.all_to_all(picked, 'gz', split_axis=0, concat_axis=0, tiled=True)  56 us
    unnamed x1, blocking collectives  28.6 us
    ppermute x1, waiting for transfers between devices, local(): before = lax.ppermute(summed[2], 'gy', up_y)  22.4 us
    pallas_call x1, Pallas kernels, local(): call(product_kernel, (9, 192, 2304), [SMEM, VMEM, VMEM, VMEM], [pltpu.VME...  16.2 us
    all_to_all x1, starting transfers between devices, local(): rows = lax.all_to_all(chunks, 'gz', split_axis=0, concat_axis=0, tiled=True)  15.2 us
    ppermute x1, waiting for transfers between devices, local(): before = lax.ppermute(summed[64:128], 'gz', up_z)  11.1 us
    ppermute x1, waiting for transfers between devices, local(): lax.ppermute(wide[:, 1:2], 'gy', up_y)  8.51 us
    convert_element_type x3, local copies, waits for them, and re-layouts, widened(): field = field.reshape(192, 4, 768).astype(F32)  6.33 us
  transfers between devices with their start and end apart: 11, of which 9 were waited for; matrix products, arithmetic and copies ran while one was open for 4% of the time, Pallas kernels for 0%

profile of v1, /device:TPU:2, one launch (start us, length us, event | category | flops | bytes accessed | tf_op | source)
XLA Modules:
  0.0 246.4 jit_solution(4097246946359224584)
XLA Ops:
  0.1 0.1 xor.34
  0.2 0.1 xor.37
  0.4 0.1 xor.40
  0.5 0.8 lt.82
  1.3 0.1 lt.85
  1.4 0.8 reshape.194
  2.2 0.5 add_select_fusion.spot_ref
  2.7 2.5 %shard_map.73.own_ref = bf16[8,64,512]{2,1,0:T(8,128)(2,1)} custom-call(s32[64]{0:T(128)} %add_select_fusion.spot_ref, bf16[8,64,512]{2,1,0:T(8,128)(2,1)} %bitcast.36), custom_call_target="tpu_custom_call" | custom-call | tf_op jit(solution)/shard_map/pallas_call | solution.py:252
  5.2 1.1 fusion.15
  6.3 3.5 %collective-permute-start = (bf16[2,2,1,64,512]{4,3,2,1,0:T(8,128)(2,1)S(1)}, bf16[2,2,1,64,512]{4,3,2,1,0:T(8,128)(2,1)S(1)}, u32[]{:S(2)}, u32[]{:S(2)}) collective-permute-start(bf16[2,2,1,64,512]{4,3,2,1,0:T(8,128)(2,1)S(1)} %get-tuple-element.17), channel_id=1, source_target_pairs={{0,1},{1,2},{2,3},{3,4},{4,5},{5,6},{6,7},{7,8},{8,9},{9,10},{10,1... | collective-permute-start | bytes 786440 | tf_op jit(solution)/shard_map/ppermute | solution.py:259
  9.9 1.3 collective-permute-start.1
  11.2 4.2 %collective-permute-done = bf16[2,2,1,64,512]{4,3,2,1,0:T(8,128)(2,1)S(1)} collective-permute-done((bf16[2,2,1,64,512]{4,3,2,1,0:T(8,128)(2,1)S(1)}, bf16[2,2,1,64,512]{4,3,2,1,0:T(8,128)(2,1)S(1)}, u32[]{:S(2)}, u32[]{:S(2)}) %collective-permute-start) | collective-permute-done | bytes 262176 | tf_op jit(solution)/shard_map/ppermute | solution.py:259
  15.4 4.1 %collective-permute-done.1 = bf16[2,2,1,64,512]{4,3,2,1,0:T(8,128)(2,1)S(1)} collective-permute-done((bf16[2,2,1,64,512]{4,3,2,1,0:T(8,128)(2,1)S(1)}, bf16[2,2,1,64,512]{4,3,2,1,0:T(8,128)(2,1)S(1)}, u32[]{:S(2)}, u32[]{:S(2)}) %collective-permute-start.1) | collective-permute-done | bytes 262176 | tf_op jit(solution)/shard_map/ppermute | solution.py:261
  19.5 1.2 pad_maximum_fusion.2
  20.8 3.4 %collective-permute-start.2 = (bf16[2,1,4,64,512]{4,3,2,1,0:T(8,128)(2,1)S(1)}, bf16[2,1,4,64,512]{4,3,2,1,0:T(8,128)(2,1)S(1)}, u32[]{:S(2)}, u32[]{:S(2)}) collective-permute-start(bf16[2,1,4,64,512]{4,3,2,1,0:T(8,128)(2,1)S(1)} %get-tuple-element.15), channel_id=1, source_target_pairs={{0,32},{32,64},{64,96},{1,33},{33,65},{65,97},{2,34},{34,66},{66,9... | collective-permute-start | bytes 1572872 | tf_op jit(solution)/shard_map/ppermute | solution.py:267
  24.1 2.5 %collective-permute-start.3 = (bf16[2,1,4,64,512]{4,3,2,1,0:T(8,128)(2,1)S(1)}, bf16[2,1,4,64,512]{4,3,2,1,0:T(8,128)(2,1)S(1)}, u32[]{:S(2)}, u32[]{:S(2)}) collective-permute-start(bf16[2,1,4,64,512]{4,3,2,1,0:T(8,128)(2,1)S(1)} %get-tuple-element.16), channel_id=1, source_target_pairs={{32,0},{64,32},{96,64},{33,1},{65,33},{97,65},{34,2},{66,34},{98,6... | collective-permute-start | bytes 1572872 | tf_op jit(solution)/shard_map/ppermute | solution.py:269
  26.7 8.5 %collective-permute-done.2 = bf16[2,1,4,64,512]{4,3,2,1,0:T(8,128)(2,1)S(1)} collective-permute-done((bf16[2,1,4,64,512]{4,3,2,1,0:T(8,128)(2,1)S(1)}, bf16[2,1,4,64,512]{4,3,2,1,0:T(8,128)(2,1)S(1)}, u32[]{:S(2)}, u32[]{:S(2)}) %collective-permute-start.2) | collective-permute-done | bytes 524320 | tf_op jit(solution)/shard_map/ppermute | solution.py:267
  35.2 3.1 %collective-permute-done.3 = bf16[2,1,4,64,512]{4,3,2,1,0:T(8,128)(2,1)S(1)} collective-permute-done((bf16[2,1,4,64,512]{4,3,2,1,0:T(8,128)(2,1)S(1)}, bf16[2,1,4,64,512]{4,3,2,1,0:T(8,128)(2,1)S(1)}, u32[]{:S(2)}, u32[]{:S(2)}) %collective-permute-start.3) | collective-permute-done | bytes 524320 | tf_op jit(solution)/shard_map/ppermute | solution.py:269
  38.3 0.3 pad_maximum_fusion.1
  38.6 1.1 slice_select_fusion.1
  39.7 0.1 div.55
  39.8 0.1 div.58
  39.8 0.1 rem.151
  40.0 0.1 ne.198
  40.0 0.1 ne.201
  40.6 0.1 lt.73
  40.8 0.1 lt.76
  40.9 0.6 fusion.8.spot_ref
  41.5 1.1 collective-permute-done.4
  42.5 0.1 broadcast_select_fusion.3
  42.7 2.4 pad_maximum_fusion
  45.0 16.2 %shard_map.74 = bf16[9,192,2304]{2,1,0:T(8,128)(2,1)} custom-call(s32[256]{0:T(256)} %fusion.8.spot_ref, bf16[8,64,2048]{2,1,0:T(8,128)(2,1)} %bitcast.33, bf16[64,64,512]{2,1,0:T(8,128)(2,1)} %bitcast.27, bf16[8,64,512]{2,1,0:T(8,128)(2,1)} %shard_map.73.own_ref), custom_call_target="tpu_custom_call" | custom-call | tf_op jit(solution)/shard_map/pallas_call | solution.py:288
  61.3 2.8 %slice_select_fusion = bf16[3,192,2304]{2,1,0:T(8,128)(2,1)S(1)} fusion(bf16[9,192,2304]{2,1,0:T(8,128)(2,1)} %shard_map.74, pred[]{:T(512)S(6)} %eq.28), kind=kLoop, calls=%fused_computation.3 | loop fusion | flops 1327104 | bytes 7962625 | tf_op jit(solution)/shard_map/jit(_where)/select_n | solution.py:309
  64.1 0.4 collective-permute-start.5
  64.5 4.9 %collective-permute-done.5 = bf16[3,192,2304]{2,1,0:T(8,128)(2,1)S(1)} collective-permute-done((bf16[3,192,2304]{2,1,0:T(8,128)(2,1)S(1)}, bf16[3,192,2304]{2,1,0:T(8,128)(2,1)S(1)}, u32[]{:S(2)}, u32[]{:S(2)}) %collective-permute-start.5) | collective-permute-done | bytes 2654240 | tf_op jit(solution)/shard_map/ppermute | solution.py:309
  69.3 2.4 broadcast_select_fusion.1
  71.8 0.7 add_convert_fusion
  72.4 1.2 slice_bitcast_fusion.1
  73.7 3.1 %collective-permute-start.6 = (bf16[192,3072]{1,0:T(8,128)(2,1)}, bf16[192,3072]{1,0:T(8,128)(2,1)}, u32[]{:S(2)}, u32[]{:S(2)}) collective-permute-start(bf16[192,3072]{1,0:T(8,128)(2,1)} %get-tuple-element.7), channel_id=1, source_target_pairs={{0,32},{32,64},{64,96},{1,33},{33,65},{65,97},{2,34},{34,66},{66,9... | collective-permute-start | bytes 3538952 | tf_op jit(solution)/shard_map/ppermute | solution.py:317
  76.8 3.7 %collective-permute-start.7 = (bf16[192,3072]{1,0:T(8,128)(2,1)S(1)}, bf16[192,3072]{1,0:T(8,128)(2,1)}, u32[]{:S(2)}, u32[]{:S(2)}) collective-permute-start(bf16[192,3072]{1,0:T(8,128)(2,1)S(1)} %get-tuple-element.8), channel_id=1, source_target_pairs={{32,0},{64,32},{96,64},{33,1},{65,33},{97,65},{34,2},{66,34},{98,6... | collective-permute-start | bytes 3538952 | tf_op jit(solution)/shard_map/ppermute | solution.py:318
  80.5 0.9 convert_element_type.36
  81.5 22.4 %collective-permute-done.6 = bf16[192,3072]{1,0:T(8,128)(2,1)} collective-permute-done((bf16[192,3072]{1,0:T(8,128)(2,1)}, bf16[192,3072]{1,0:T(8,128)(2,1)}, u32[]{:S(2)}, u32[]{:S(2)}) %collective-permute-start.6) | collective-permute-done | bytes 1179680 | tf_op jit(solution)/shard_map/ppermute | solution.py:317
  103.9 2.7 %convert_element_type.35 = bf16[192,4,768]{2,1,0:T(4,128)(2,1)S(1)} reshape(bf16[192,3072]{1,0:T(8,128)(2,1)} %collective-permute-done.6) | data formatting | bytes 2359296 | tf_op jit(solution)/shard_map/convert_element_type | solution.py:321
  106.6 2.7 %convert_element_type.37 = bf16[192,4,768]{2,1,0:T(4,128)(2,1)S(1)} reshape(bf16[192,3072]{1,0:T(8,128)(2,1)} %collective-permute-done.7) | data formatting | bytes 2359296 | tf_op jit(solution)/shard_map/convert_element_type | solution.py:321
  109.3 1.5 add_convert_fusion.1
  110.8 0.7 fusion.13
  111.6 3.6 %collective-permute-start.8 = (bf16[64,5120]{1,0:T(8,128)(2,1)S(1)}, bf16[64,5120]{1,0:T(8,128)(2,1)S(1)}, u32[]{:S(2)}, u32[]{:S(2)}) collective-permute-start(bf16[64,5120]{1,0:T(8,128)(2,1)S(1)} %bitcast.34), channel_id=1, source_target_pairs={{0,1},{1,2},{2,3},{3,4},{4,5},{5,6},{6,7},{7,8},{8,9},{9,10},{10,1... | collective-permute-start | bytes 1966088 | tf_op jit(solution)/shard_map/ppermute | solution.py:327
  115.2 1.3 collective-permute-start.9
  116.5 0.9 copy.11
  117.4 11.1 %collective-permute-done.8.before_ref = bf16[64,5120]{1,0:T(8,128)(2,1)S(1)} collective-permute-done((bf16[64,5120]{1,0:T(8,128)(2,1)S(1)}, bf16[64,5120]{1,0:T(8,128)(2,1)S(1)}, u32[]{:S(2)}, u32[]{:S(2)}) %collective-permute-start.8) | collective-permute-done | bytes 655392 | tf_op jit(solution)/shard_map/ppermute | solution.py:327
  128.5 4.2 %collective-permute-done.9.after_ref = bf16[64,5120]{1,0:T(8,128)(2,1)S(1)} collective-permute-done((bf16[64,5120]{1,0:T(8,128)(2,1)S(1)}, bf16[64,5120]{1,0:T(8,128)(2,1)S(1)}, u32[]{:S(2)}, u32[]{:S(2)}) %collective-permute-start.9) | collective-permute-done | bytes 655392 | tf_op jit(solution)/shard_map/ppermute | solution.py:328
  132.8 0.8 copy-done.3
  133.6 3.2 %shard_map.75 = bf16[32,64,256]{2,1,0:T(8,128)(2,1)} custom-call(s32[1]{0:T(128)} %bitcast.2.side_ref, bf16[64,5120]{1,0:T(8,128)(2,1)} %bitcast.29, bf16[64,5120]{1,0:T(8,128)(2,1)} %copy-done.2, bf16[64,5120]{1,0:T(8,128)(2,1)} %copy-done.3), custom_call_target="tpu_custom_call" | custom-call | tf_op jit(solution)/shard_map/pallas_call | solution.py:330
  136.8 15.2 %all-to-all-start = ((bf16[32,64,256]{2,1,0:T(8,128)(2,1)}), bf16[32,64,256]{2,1,0:T(8,128)(2,1)S(1)}, u32[]{:S(2)}, u32[]{:S(2)}) async-start(bf16[32,64,256]{2,1,0:T(8,128)(2,1)} %shard_map.75), calls=%async_computation | async-start | bytes 2097152 | tf_op jit(solution)/shard_map/all_to_all | solution.py:334
  152.7 0.7 dynamic-slice
  153.4 0.7 bitcast_dynamic-update-slice_fusion
  154.1 28.6 %all-reduce.5 = s32[32]{0:T(128)S(1)} all-reduce(s32[32]{0:T(128)S(1)} %bitcast_dynamic-update-slice_fusion), channel_id=2, replica_groups=mesh['gx'=2,'gy'=4,'gz'=32] {'gz'}, use_global_device_ids=true, to_apply=%add.5 | all-reduce | flops 32 | bytes 256
  182.7 0.1 fusion
  182.8 0.5 convert_element_type.33.live_ref
  183.3 0.6 select_reduce_fusion.from_ref
  183.9 1.0 copy-done.1
  184.9 4.1 %shard_map.76 = bf16[64,64,256]{2,1,0:T(8,128)(2,1)} custom-call(s32[64]{0:T(128)} %select_reduce_fusion.from_ref, s32[64]{0:T(128)} %convert_element_type.33.live_ref, bf16[32,64,256]{2,1,0:T(8,128)(2,1)} %copy-done.1), custom_call_target="tpu_custom_call" | custom-call | tf_op jit(solution)/shard_map/pallas_call | solution.py:335
  189.0 56.0 %all_to_all.10 = bf16[64,64,256]{2,1,0:T(8,128)(2,1)S(1)} all-to-all(bf16[64,64,256]{2,1,0:T(8,128)(2,1)} %shard_map.76), channel_id=1, replica_groups=mesh['gx'=2,'gy'=4,'gz'=32] {'gz'}, dimensions={0} | all-to-all | bytes 4194304 | tf_op jit(solution)/shard_map/all_to_all | solution.py:336
  244.9 1.5 copy.10
  (39 shorter events, 1.1 us)
Async XLA Ops:
  5.2 33.1 %copy-start = (bf16[8,64,512]{2,1,0:T(8,128)(2,1)S(1)}, bf16[8,64,512]{2,1,0:T(8,128)(2,1)}, u32[]{:S(2)}) copy-start(bf16[8,64,512]{2,1,0:T(8,128)(2,1)} %shard_map.73.own_ref) | copy-start | bytes 1572868
  6.3 9.0 %collective-permute-start = (bf16[2,2,1,64,512]{4,3,2,1,0:T(8,128)(2,1)S(1)}, bf16[2,2,1,64,512]{4,3,2,1,0:T(8,128)(2,1)S(1)}, u32[]{:S(2)}, u32[]{:S(2)}) collective-permute-start(bf16[2,2,1,64,512]{4,3,2,1,0:T(8,128)(2,1)S(1)} %get-tuple-element.17), channel_id=1, source_target_pairs={{0,1},{1,2},{2,3},{3,4},{4,5},{5,6},{6,7},{7,8},{8,9},{9,10},{10,1... | collective-permute-start | bytes 786440 | tf_op jit(solution)/shard_map/ppermute | solution.py:259
  9.9 9.7 %collective-permute-start.1 = (bf16[2,2,1,64,512]{4,3,2,1,0:T(8,128)(2,1)S(1)}, bf16[2,2,1,64,512]{4,3,2,1,0:T(8,128)(2,1)S(1)}, u32[]{:S(2)}, u32[]{:S(2)}) collective-permute-start(bf16[2,2,1,64,512]{4,3,2,1,0:T(8,128)(2,1)S(1)} %get-tuple-element.18), channel_id=1, source_target_pairs={{1,0},{2,1},{3,2},{4,3},{5,4},{6,5},{7,6},{8,7},{9,8},{10,9},{11,1... | collective-permute-start | bytes 786440 | tf_op jit(solution)/shard_map/ppermute | solution.py:261
  20.8 14.4 %collective-permute-start.2 = (bf16[2,1,4,64,512]{4,3,2,1,0:T(8,128)(2,1)S(1)}, bf16[2,1,4,64,512]{4,3,2,1,0:T(8,128)(2,1)S(1)}, u32[]{:S(2)}, u32[]{:S(2)}) collective-permute-start(bf16[2,1,4,64,512]{4,3,2,1,0:T(8,128)(2,1)S(1)} %get-tuple-element.15), channel_id=1, source_target_pairs={{0,32},{32,64},{64,96},{1,33},{33,65},{65,97},{2,34},{34,66},{66,9... | collective-permute-start | bytes 1572872 | tf_op jit(solution)/shard_map/ppermute | solution.py:267
  24.1 14.1 %collective-permute-start.3 = (bf16[2,1,4,64,512]{4,3,2,1,0:T(8,128)(2,1)S(1)}, bf16[2,1,4,64,512]{4,3,2,1,0:T(8,128)(2,1)S(1)}, u32[]{:S(2)}, u32[]{:S(2)}) collective-permute-start(bf16[2,1,4,64,512]{4,3,2,1,0:T(8,128)(2,1)S(1)} %get-tuple-element.16), channel_id=1, source_target_pairs={{32,0},{64,32},{96,64},{33,1},{65,33},{97,65},{34,2},{66,34},{98,6... | collective-permute-start | bytes 1572872 | tf_op jit(solution)/shard_map/ppermute | solution.py:269
  26.7 13.0 %copy-start.4 = (s32[2,2,2,32]{3,2,1,0:T(2,128)S(1)}, s32[2,2,2,32]{3,2,1,0:T(2,128)}, u32[]{:S(2)}) copy-start(s32[2,2,2,32]{3,2,1,0:T(2,128)} %param.8) | copy-start | bytes 3076
  38.6 2.0 copy-start.5
  39.7 2.9 %collective-permute-start.4 = (bf16[1,4,4,64,512]{4,3,2,1,0:T(8,128)(2,1)}, bf16[1,4,4,64,512]{4,3,2,1,0:T(8,128)(2,1)S(1)}, u32[]{:S(2)}, u32[]{:S(2)}) collective-permute-start(bf16[1,4,4,64,512]{4,3,2,1,0:T(8,128)(2,1)} %slice_select_fusion.1), channel_id=1, source_target_pairs={{0,128},{128,0},{1,129},{129,1},{2,130},{130,2},{3,131},{131,3},{4... | collective-permute-start | bytes 3145736 | tf_op jit(solution)/shard_map/ppermute | solution.py:273
  64.1 5.2 %collective-permute-start.5 = (bf16[3,192,2304]{2,1,0:T(8,128)(2,1)S(1)}, bf16[3,192,2304]{2,1,0:T(8,128)(2,1)S(1)}, u32[]{:S(2)}, u32[]{:S(2)}) collective-permute-start(bf16[3,192,2304]{2,1,0:T(8,128)(2,1)S(1)} %slice_select_fusion), channel_id=1, source_target_pairs={{0,128},{128,0},{1,129},{129,1},{2,130},{130,2},{3,131},{131,3},{4... | collective-permute-start | bytes 7962632 | tf_op jit(solution)/shard_map/ppermute | solution.py:309
  73.7 30.2 %collective-permute-start.6 = (bf16[192,3072]{1,0:T(8,128)(2,1)}, bf16[192,3072]{1,0:T(8,128)(2,1)}, u32[]{:S(2)}, u32[]{:S(2)}) collective-permute-start(bf16[192,3072]{1,0:T(8,128)(2,1)} %get-tuple-element.7), channel_id=1, source_target_pairs={{0,32},{32,64},{64,96},{1,33},{33,65},{65,97},{2,34},{34,66},{66,9... | collective-permute-start | bytes 3538952 | tf_op jit(solution)/shard_map/ppermute | solution.py:317
  76.8 29.8 %collective-permute-start.7 = (bf16[192,3072]{1,0:T(8,128)(2,1)S(1)}, bf16[192,3072]{1,0:T(8,128)(2,1)}, u32[]{:S(2)}, u32[]{:S(2)}) collective-permute-start(bf16[192,3072]{1,0:T(8,128)(2,1)S(1)} %get-tuple-element.8), channel_id=1, source_target_pairs={{32,0},{64,32},{96,64},{33,1},{65,33},{97,65},{34,2},{66,34},{98,6... | collective-permute-start | bytes 3538952 | tf_op jit(solution)/shard_map/ppermute | solution.py:318
  111.6 17.0 %collective-permute-start.8 = (bf16[64,5120]{1,0:T(8,128)(2,1)S(1)}, bf16[64,5120]{1,0:T(8,128)(2,1)S(1)}, u32[]{:S(2)}, u32[]{:S(2)}) collective-permute-start(bf16[64,5120]{1,0:T(8,128)(2,1)S(1)} %bitcast.34), channel_id=1, source_target_pairs={{0,1},{1,2},{2,3},{3,4},{4,5},{5,6},{6,7},{7,8},{8,9},{9,10},{10,1... | collective-permute-start | bytes 1966088 | tf_op jit(solution)/shard_map/ppermute | solution.py:327
  115.2 17.5 %collective-permute-start.9 = (bf16[64,5120]{1,0:T(8,128)(2,1)S(1)}, bf16[64,5120]{1,0:T(8,128)(2,1)S(1)}, u32[]{:S(2)}, u32[]{:S(2)}) collective-permute-start(bf16[64,5120]{1,0:T(8,128)(2,1)S(1)} %bitcast.35), channel_id=1, source_target_pairs={{1,0},{2,1},{3,2},{4,3},{5,4},{6,5},{7,6},{8,7},{9,8},{10,9},{11,1... | collective-permute-start | bytes 1966088 | tf_op jit(solution)/shard_map/ppermute | solution.py:328
  117.4 35.3 %copy-start.6 = (u32[256]{0:T(256)S(1)}, u32[256]{0:T(256)}, u32[]{:S(2)}) copy-start(u32[256]{0:T(256)} %constant.153) | copy-start | bytes 3076
  128.5 4.2 %copy-start.2 = (bf16[64,5120]{1,0:T(8,128)(2,1)}, bf16[64,5120]{1,0:T(8,128)(2,1)S(1)}, u32[]{:S(2)}) copy-start(bf16[64,5120]{1,0:T(8,128)(2,1)S(1)} %collective-permute-done.8.before_ref) | copy-start | bytes 1966084
  132.8 0.8 copy-start.3
  136.8 47.1 %all-to-all-start = ((bf16[32,64,256]{2,1,0:T(8,128)(2,1)}), bf16[32,64,256]{2,1,0:T(8,128)(2,1)S(1)}, u32[]{:S(2)}, u32[]{:S(2)}) async-start(bf16[32,64,256]{2,1,0:T(8,128)(2,1)} %shard_map.75), calls=%async_computation | async-start | bytes 2097152 | tf_op jit(solution)/shard_map/all_to_all | solution.py:334
  183.9 1.0 copy-start.1
